TPU v7x, 32 devices: a whole 2x2x4 slice. The times are simulated.
32 devices in a mesh: rows: 8 (over y, x, core), cols: 4 (over z).
Axes of the slice: x: 2, y: 2, z: 4, core: 2. Of those that a mesh axis runs over, the one named last changes fastest.
Arguments:
- embeddings: bfloat16 [12288, 128], P('rows'), may hold values from -6 to 6
- length_scale: bfloat16 [12288], P('rows'), may hold values from 0.25 to 0.69921875
- start_vectors: float32 [128, 12288], P('cols', 'rows'), may hold values from -6 to 6
- neighbour_ids: int32 [48, 12], P('rows'), may hold values from 0 to 47, as said below
- neighbour_counts: int32 [48], P('rows'), may hold values from 1 to 12
Outputs:
- basis: float32 [128, 12288], P('cols', 'rows')
Inputs may be any that keep to these rules, and one draw needn't show every extreme that they name: `neighbour_ids`: slot 0 of a row block names the block itself; the slots from neighbour_counts on repeat the block itself and are unused; the used ids of one block are distinct and name blocks held by the same index of rows or by an index one away along rows.
All inputs are finite; a program needn't handle non-finite values.
Results may differ from a plain program's by a relative error of at most 0.0003.
Values may be sent and summed in bfloat16 or wider, within the bound.
A program may use at most 64 MiB of HBM per device.

v0:
```python
import functools

import jax
import jax.numpy as jnp
from jax import lax
from jax.experimental import pallas as pl
from jax.experimental.pallas import tpu as pltpu
from jax.sharding import PartitionSpec as P

ITERS = 3
GROUP = 4
F32 = jnp.float32
BF16 = jnp.bfloat16
highest = lax.Precision.HIGHEST
VMEM = pl.BlockSpec(memory_space=pltpu.VMEM)
SMEM = pl.BlockSpec(memory_space=pltpu.SMEM)
NT = (((1,), (1,)), ((), ()))


def passed_along(value, axis, steps):
    count = lax.axis_size(axis)
    leading, last = (max(0, -steps), min(count, count - steps))
    return lax.ppermute(value, axis, [(source, source + steps) for source in range(leading, last)])


def split(value):
    high = value.astype(BF16)
    return high, (value - high.astype(F32)).astype(BF16)


def features(emb, left_side):
    size, width = emb.shape
    wide = emb.astype(F32)
    norm = jnp.sum(wide * wide, axis=1, keepdims=True)
    part0 = norm.astype(BF16).astype(F32)
    part1 = (norm - part0).astype(BF16).astype(F32)
    part2 = norm - part0 - part1
    lane = lax.broadcasted_iota(jnp.int32, (size, width), 1)
    base = 3 if left_side else 0
    ones = jnp.where((lane >= 3 - base) & (lane < 6 - base), 1.0, 0.0)
    side = jnp.where(lane == base, -part0, ones)
    side = jnp.where(lane == base + 1, -part1, side)
    side = jnp.where(lane == base + 2, -part2, side)
    main = wide if left_side else 2.0 * wide
    return jnp.concatenate([main.astype(BF16), side.astype(BF16)], axis=1)


def rate_of(spread, width):
    return (1.4426950408889634 / (2.0 * width)) ** 0.5 / spread


def listing(ids, counts, row_here, rows, cols, near):
    blocks, slots = ids.shape
    first = row_here * blocks
    total = jnp.int32(0)
    for b in range(blocks):
        count = counts[b]
        for s in range(slots):
            gap = ids[b, s] - first
            inside = (gap >= 0) & (gap < blocks)
            wanted = inside if near else jnp.logical_not(inside)
            rows[total] = b
            cols[total] = gap if near else jnp.where(gap < 0, gap + blocks, gap)
            total = total + jnp.where(wanted & (s < count), 1, 0)
    for pad in range(GROUP):
        rows[total + pad] = 0
        cols[total + pad] = 0
    return total


def tiles_kernel(near, *refs):
    if near:
        (here, ids, counts, emb, spread, tiles, degree, rows, cols, groups,
         left, left_rate, right) = refs
        far_set = [(emb, spread)]
    else:
        (here, ids, counts, emb, spread, emb_l, spread_l, emb_r, spread_r, near_degree, start,
         tiles, scale, panel, weighted, rows, cols, groups, left, left_rate, right, degree) = refs
        far_set = [(emb_l, spread_l), (emb_r, spread_r)]
    blocks, size, width = emb.shape
    total = listing(ids, counts, here[0], rows, cols, near)
    groups[0] = (total + GROUP - 1) // GROUP
    for b in range(blocks):
        right[b] = features(emb[b], False)
    position = 0
    for far_emb, far_spread in far_set:
        for b in range(blocks):
            left[position] = features(far_emb[b], True)
            rate = rate_of(far_spread[b].astype(F32), width)
            left_rate[position] = jnp.broadcast_to(rate, (128, size)).T
            position += 1
    degree[...] = jnp.zeros(degree.shape, F32) if near else near_degree[...]
    if near:
        apart = lax.broadcasted_iota(jnp.int32, (size, size), 0) != lax.broadcasted_iota(
            jnp.int32, (size, size), 1
        )

    def one(t, carry):
        b, c = rows[t], cols[t]
        gap = lax.dot_general(left[c], right[b], NT, preferred_element_type=F32)
        rate = left_rate[c]
        own = rate_of(spread[b].astype(F32), width)
        tile = jnp.exp2(gap * jnp.concatenate([rate] * (size // 128), axis=1) * own)
        if near:
            tile = jnp.where(apart | (b != c), tile, 0.0)
        degree[b] += jnp.sum(tile, axis=0, keepdims=True)
        high, low = split(tile)
        tiles[t, :size] = high
        tiles[t, size:] = low
        return carry

    lax.fori_loop(0, total, one, 0)
    for pad in range(GROUP - 1):
        tiles[total + pad] = jnp.zeros((2 * size, size), BF16)
    if not near:
        count = start.shape[0]
        for b in range(blocks):
            factor = 1.0 / jnp.sqrt(degree[b])
            scale[b] = factor
            vecs = start[:, b * size:(b + 1) * size]
            panel[b] = vecs
            high, low = split(vecs * factor)
            weighted[b, :count] = high
            weighted[b, count:] = low


def add_products(rows, cols, groups, tiles, vectors, total):
    count, size = total.shape[1:]

    def one(group, carry):
        found = []
        for place in range(GROUP):
            t = group * GROUP + place
            both = vectors[cols[t]]
            out = jnp.dot(both, tiles[t, :size], preferred_element_type=F32)
            more = jnp.dot(both[:count], tiles[t, size:], preferred_element_type=F32)
            found.append((rows[t], out[:count] + out[count:] + more))
        for b, value in found:
            total[b] += value
        return carry

    lax.fori_loop(0, groups[0], one, 0)


def near_product_kernel(rows, cols, groups, tiles, weighted, product):
    product[...] = jnp.zeros(product.shape, F32)
    add_products(rows, cols, groups, tiles, weighted, product)


def far_product_kernel(final, rows, cols, groups, tiles, from_left, from_right, near, scale,
                       panel, *rest):
    if final:
        out, vectors, total = rest
    else:
        out, weighted, vectors, total = rest
    blocks, count, size = panel.shape
    for b in range(blocks):
        vectors[b] = from_left[b]
        vectors[blocks + b] = from_right[b]
    total[...] = near[...]
    add_products(rows, cols, groups, tiles, vectors, total)
    for b in range(blocks):
        factor = scale[b]
        vecs = 0.5 * (panel[b] + factor * total[b])
        if final:
            out[:, b * size:(b + 1) * size] = vecs
        else:
            out[b] = vecs
            high, low = split(vecs * factor)
            weighted[b, :count] = high
            weighted[b, count:] = low


def params():
    return pltpu.CompilerParams(vmem_limit_bytes=20 << 20)


def local(embeddings, length_scale, start_vectors, neighbour_ids, neighbour_counts):
    blocks, slots = neighbour_ids.shape
    points, width = embeddings.shape
    size = points // blocks
    count = start_vectors.shape[0]
    here = lax.axis_index("rows").astype(jnp.int32).reshape(1)
    col_here = lax.axis_index("cols")
    shape = jax.ShapeDtypeStruct
    emb = embeddings.reshape(blocks, size, width)
    spread = length_scale.reshape(blocks, 1, size)
    sides = [passed_along((emb, spread), "rows", step) for step in (1, -1)]
    near_max = blocks * min(slots, blocks) + GROUP
    far_max = blocks * (slots - 1) + GROUP

    def lists(extent):
        return [shape((extent,), jnp.int32), shape((extent,), jnp.int32), shape((1,), jnp.int32)]

    def work(sets):
        return [
            pltpu.VMEM((sets * blocks, size, 2 * width), BF16),
            pltpu.VMEM((sets * blocks, size, 128), F32),
            pltpu.VMEM((blocks, size, 2 * width), BF16),
        ]

    def tile_cost(number):
        return pl.CostEstimate(
            flops=number * size * size * 2 * width * 2, transcendentals=number * size * size,
            bytes_accessed=number * size * size * 4)

    near_tiles, near_degree, near_rows, near_cols, near_groups = pl.pallas_call(
        functools.partial(tiles_kernel, True),
        out_shape=[pltpu.VMEM((near_max, 2 * size, size), BF16), shape((blocks, 1, size), F32)]
        + lists(near_max),
        in_specs=[SMEM] * 3 + [VMEM] * 2,
        out_specs=[VMEM] * 2 + [SMEM] * 3,
        scratch_shapes=work(1),
        compiler_params=params(),
        cost_estimate=tile_cost(20),
        name="near_tiles",
    )(here, neighbour_ids, neighbour_counts, emb, spread)
    block_f32 = shape((blocks, count, size), F32)
    block_both = shape((blocks, 2 * count, size), BF16)
    far_tiles, scale, panel, weighted, far_rows, far_cols, far_groups = pl.pallas_call(
        functools.partial(tiles_kernel, False),
        out_shape=[pltpu.VMEM((far_max, 2 * size, size), BF16), shape((blocks, 1, size), F32),
                   block_f32, block_both] + lists(far_max),
        in_specs=[SMEM] * 3 + [VMEM] * 8,
        out_specs=[VMEM] * 4 + [SMEM] * 3,
        scratch_shapes=work(2) + [pltpu.VMEM((blocks, 1, size), F32)],
        compiler_params=params(),
        cost_estimate=tile_cost(30),
        name="far_tiles",
    )(here, neighbour_ids, neighbour_counts, emb, spread, *sides[0], *sides[1], near_degree,
      start_vectors)

    for iteration in range(ITERS):
        final = iteration == ITERS - 1
        from_left = passed_along(weighted, "rows", 1)
        from_right = passed_along(weighted, "rows", -1)
        near = pl.pallas_call(
            near_product_kernel,
            out_shape=block_f32,
            in_specs=[SMEM] * 3 + [VMEM] * 2,
            out_specs=VMEM,
            compiler_params=params(),
            cost_estimate=tile_cost(20),
            name="near_product",
        )(near_rows, near_cols, near_groups, near_tiles, weighted)
        done = pl.pallas_call(
            functools.partial(far_product_kernel, final),
            out_shape=[shape((count, points), F32)] if final else [block_f32, block_both],
            in_specs=[SMEM] * 3 + [VMEM] * 6,
            out_specs=[VMEM] if final else [VMEM] * 2,
            scratch_shapes=[pltpu.VMEM((2 * blocks, 2 * count, size), BF16),
                            pltpu.VMEM((blocks, count, size), F32)],
            compiler_params=params(),
            cost_estimate=tile_cost(30),
            name="far_product",
        )(far_rows, far_cols, far_groups, far_tiles, from_left, from_right, near, scale, panel)
        if final:
            flat = done[0]
        else:
            panel, weighted = done
    flat_vecs = lax.all_gather(flat, "cols", axis=0, tiled=True)
    columns = flat_vecs.shape[0]
    total_points = points * lax.axis_size("rows")
    gram_mat = lax.psum(jnp.dot(flat_vecs, flat_vecs.T, precision=highest), "rows")
    gram_mat = gram_mat / total_points
    low_factor = jnp.linalg.cholesky(gram_mat)
    inverse = lax.linalg.triangular_solve(
        low_factor, jnp.eye(columns, dtype=F32), left_side=True, lower=True
    )
    rows_mine = lax.dynamic_slice_in_dim(inverse, col_here * count, count, 0)
    return jnp.dot(rows_mine, flat_vecs, precision=highest)


def solution(mesh):
    placed = (P("rows", None), P("rows"), P("cols", "rows"), P("rows", None), P("rows"))
    return jax.shard_map(
        local, mesh=mesh, in_specs=placed, out_specs=P("cols", "rows"), check_vma=False
    )
```

profile of v0, /device:TPU:0, one launch (start us, length us, event | category | flops | bytes accessed | tf_op | source)
XLA Modules:
  0.0 190.6 jit_solution(10481273207926182662)
XLA Ops:
  6.5 1.3 collective-permute-start.2
  7.8 3.1 %collective-permute-start = (bf16[6,256,128]{2,1,0:T(8,128)(2,1)}, bf16[6,256,128]{2,1,0:T(8,128)(2,1)S(1)}, u32[]{:S(2)}, u32[]{:S(2)}) collective-permute-start(bf16[6,256,128]{2,1,0:T(8,128)(2,1)} %bitcast.15), channel_id=1, source_target_pairs={{0,4},{4,8},{8,12},{12,16},{16,20},{20,24},{24,28},{1,5},{5,9},{9,... | collective-permute-start | bytes 1179656 | tf_op jit(solution)/shard_map/ppermute | solution.py:23
  10.9 0.7 reshape.21.refs_4_
  11.6 1.3 collective-permute-start.3
  12.9 5.1 %collective-permute-start.1 = (bf16[6,1,256]{2,1,0:T(2,128)(2,1)S(1)}, bf16[6,1,256]{2,1,0:T(2,128)(2,1)S(1)}, u32[]{:S(2)}, u32[]{:S(2)}) collective-permute-start(bf16[6,1,256]{2,1,0:T(2,128)(2,1)S(1)} %reshape.21.refs_4_), channel_id=1, source_target_pairs={{0,4},{4,8},{8,12},{12,16},{16,20},{20,24},{24,28},{1,5},{5,9},{9,... | collective-permute-start | bytes 9224 | tf_op jit(solution)/shard_map/ppermute | solution.py:23
  18.0 0.0 copy-start.2
  18.0 1.0 copy-done.2
  19.0 0.7 copy-done.4
  19.7 0.7 copy-done.5
  20.3 10.3 %near_tiles.1 = (bf16[40,512,256]{2,1,0:T(8,128)(2,1)S(1)}, f32[6,1,256]{2,1,0:T(1,128)S(1)}, s32[40]{0:T(128)S(1)}, s32[40]{0:T(128)S(1)}, s32[1]{0:T(128)}) custom-call(s32[1]{0:T(128)} %bitcast.refs_0_, s32[6,12]{1,0:T(8,128)S(1)} %copy-done.4, s32[6]{0:T(128)S(1)} %copy-done.5, bf16[6,256,128]{2,1,0:T(8,128)(2,1)S(1)} %bitcast.16, ...), custom_call_target="tpu_custom_call" | custom-call | flops 671088640 | bytes 5242880 | tf_op jit(solution)/shard_map/near_tiles/pallas_call | solution.py:207
  30.6 4.0 %copy-done = bf16[40,512,256]{2,1,0:T(8,128)(2,1)} copy-done((bf16[40,512,256]{2,1,0:T(8,128)(2,1)}, bf16[40,512,256]{2,1,0:T(8,128)(2,1)S(1)}, u32[]{:S(2)}) %copy-start) | copy-done | bytes 10485784
  34.6 0.0 collective-permute-done.3.refs_8_
  34.6 0.0 collective-permute-done.1.refs_6_
  34.6 0.0 collective-permute-done.2.refs_7_
  34.6 0.0 collective-permute-done.refs_5_
  34.6 0.0 copy-start.3
  34.6 0.9 copy-done.3
  35.5 10.2 %far_tiles.1 = (bf16[70,512,256]{2,1,0:T(8,128)(2,1)S(1)}, f32[6,1,256]{2,1,0:T(1,128)S(1)}, f32[6,32,256]{2,1,0:T(8,128)S(1)}, bf16[6,64,256]{2,1,0:T(8,128)(2,...) custom-call(s32[1]{0:T(128)} %bitcast.refs_0_, s32[6,12]{1,0:T(8,128)S(1)} %copy-done.4, s32[6]{0:T(128)S(1)} %copy-done.5, ...), custom_call_target="tpu_custom_call" | custom-call | flops 1006632960 | bytes 7864320 | tf_op jit(solution)/shard_map/far_tiles/pallas_call | solution.py:220
  45.7 1.3 collective-permute-start.5
  47.0 3.0 %collective-permute-start.4 = (bf16[6,64,256]{2,1,0:T(8,128)(2,1)S(1)}, bf16[6,64,256]{2,1,0:T(8,128)(2,1)S(1)}, u32[]{:S(2)}, u32[]{:S(2)}) collective-permute-start(bf16[6,64,256]{2,1,0:T(8,128)(2,1)S(1)} %get-tuple-element.26.weighted), channel_id=1, source_target_pairs={{0,4},{4,8},{8,12},{12,16},{16,20},{20,24},{24,28},{1,5},{5,9},{9,... | collective-permute-start | bytes 589832 | tf_op jit(solution)/shard_map/ppermute | solution.py:23
  50.1 4.0 %copy-done.1 = bf16[40,512,256]{2,1,0:T(8,128)(2,1)S(1)} copy-done((bf16[40,512,256]{2,1,0:T(8,128)(2,1)S(1)}, bf16[40,512,256]{2,1,0:T(8,128)(2,1)}, u32[]{:S(2)}) %copy-start.1) | copy-done | bytes 10485784
  54.0 3.2 %near_product.3.near = f32[6,32,256]{2,1,0:T(8,128)S(1)} custom-call(s32[40]{0:T(128)S(1)} %get-tuple-element.27.rows, s32[40]{0:T(128)S(1)} %get-tuple-element.28.cols, s32[1]{0:T(128)} %get-tuple-element.29.groups, bf16[40,512,256]{2,1,0:T(8,128)(2,1)S(1)} %copy-done.1, bf16[6,64,256]{2,1,0:T(8,128)(2,1)S(1)} %get-tuple-element.26.weighted), custom_call_target="tpu_custom_call" | custom-call | flops 671088640 | bytes 5242880 | tf_op jit(solution)/shard_map/near_product/pallas_call | solution.py:237
  57.3 0.0 collective-permute-done.5.from_right
  57.3 0.0 collective-permute-done.4.from_left
  57.3 3.3 %far_product.3 = (f32[6,32,256]{2,1,0:T(8,128)S(1)}, bf16[6,64,256]{2,1,0:T(8,128)(2,1)S(1)}) custom-call(s32[70]{0:T(128)S(1)} %get-tuple-element.22.rows, s32[70]{0:T(128)S(1)} %get-tuple-element.23.cols, s32[1]{0:T(128)} %get-tuple-element.24.groups, bf16[70,512,256]{2,1,0:T(8,128)(2,1)S(1)} %get-tuple-element.25.tiles, ...), custom_call_target="tpu_custom_call" | custom-call | flops 1006632960 | bytes 7864320 | tf_op jit(solution)/shard_map/far_product/pallas_call | solution.py:246
  60.6 1.3 collective-permute-start.7
  61.9 3.0 %collective-permute-start.6 = (bf16[6,64,256]{2,1,0:T(8,128)(2,1)S(1)}, bf16[6,64,256]{2,1,0:T(8,128)(2,1)S(1)}, u32[]{:S(2)}, u32[]{:S(2)}) collective-permute-start(bf16[6,64,256]{2,1,0:T(8,128)(2,1)S(1)} %get-tuple-element.33.weighted), channel_id=1, source_target_pairs={{0,4},{4,8},{8,12},{12,16},{16,20},{20,24},{24,28},{1,5},{5,9},{9,... | collective-permute-start | bytes 589832 | tf_op jit(solution)/shard_map/ppermute | solution.py:23
  65.0 3.2 %near_product.4.near = f32[6,32,256]{2,1,0:T(8,128)S(1)} custom-call(s32[40]{0:T(128)S(1)} %get-tuple-element.27.rows, s32[40]{0:T(128)S(1)} %get-tuple-element.28.cols, s32[1]{0:T(128)} %get-tuple-element.29.groups, bf16[40,512,256]{2,1,0:T(8,128)(2,1)S(1)} %copy-done.1, bf16[6,64,256]{2,1,0:T(8,128)(2,1)S(1)} %get-tuple-element.33.weighted), custom_call_target="tpu_custom_call" | custom-call | flops 671088640 | bytes 5242880 | tf_op jit(solution)/shard_map/near_product/pallas_call | solution.py:237
  68.2 0.0 collective-permute-done.7.from_right
  68.2 3.3 %far_product.4 = (f32[6,32,256]{2,1,0:T(8,128)S(1)}, bf16[6,64,256]{2,1,0:T(8,128)(2,1)S(1)}) custom-call(s32[70]{0:T(128)S(1)} %get-tuple-element.22.rows, s32[70]{0:T(128)S(1)} %get-tuple-element.23.cols, s32[1]{0:T(128)} %get-tuple-element.24.groups, bf16[70,512,256]{2,1,0:T(8,128)(2,1)S(1)} %get-tuple-element.25.tiles, ...), custom_call_target="tpu_custom_call" | custom-call | flops 1006632960 | bytes 7864320 | tf_op jit(solution)/shard_map/far_product/pallas_call | solution.py:246
  71.5 1.3 collective-permute-start.9
  72.8 3.0 %collective-permute-start.8 = (bf16[6,64,256]{2,1,0:T(8,128)(2,1)S(1)}, bf16[6,64,256]{2,1,0:T(8,128)(2,1)S(1)}, u32[]{:S(2)}, u32[]{:S(2)}) collective-permute-start(bf16[6,64,256]{2,1,0:T(8,128)(2,1)S(1)} %get-tuple-element.35.weighted), channel_id=1, source_target_pairs={{0,4},{4,8},{8,12},{12,16},{16,20},{20,24},{24,28},{1,5},{5,9},{9,... | collective-permute-start | bytes 589832 | tf_op jit(solution)/shard_map/ppermute | solution.py:23
  75.9 3.2 %near_product.5.near = f32[6,32,256]{2,1,0:T(8,128)S(1)} custom-call(s32[40]{0:T(128)S(1)} %get-tuple-element.27.rows, s32[40]{0:T(128)S(1)} %get-tuple-element.28.cols, s32[1]{0:T(128)} %get-tuple-element.29.groups, bf16[40,512,256]{2,1,0:T(8,128)(2,1)S(1)} %copy-done.1, bf16[6,64,256]{2,1,0:T(8,128)(2,1)S(1)} %get-tuple-element.35.weighted), custom_call_target="tpu_custom_call" | custom-call | flops 671088640 | bytes 5242880 | tf_op jit(solution)/shard_map/near_product/pallas_call | solution.py:237
  79.1 0.0 collective-permute-done.8.from_left
  79.1 3.3 %far_product.5 = f32[32,1536]{1,0:T(8,128)S(1)} custom-call(s32[70]{0:T(128)S(1)} %get-tuple-element.22.rows, s32[70]{0:T(128)S(1)} %get-tuple-element.23.cols, s32[1]{0:T(128)} %get-tuple-element.24.groups, bf16[70,512,256]{2,1,0:T(8,128)(2,1)S(1)} %get-tuple-element.25.tiles, bf16[6,64,256]{2,1,0:T(8,128)(2,1)S(1)} %collective-permute-done.8.from_left, ...), custom_call_target="tpu_custom_call" | custom-call | flops 1006632960 | bytes 7864320 | tf_op jit(solution)/shard_map/far_product/pallas_call | solution.py:246
  82.4 18.7 %all_gather.3 = f32[128,1536]{1,0:T(8,128)S(1)} all-gather(f32[32,1536]{1,0:T(8,128)S(1)} %far_product.5), channel_id=1, replica_groups=mesh['rows'=8,'cols'=4] {'cols'}, dimensions={0}, use_global_device_ids=true | all-gather | bytes 983040 | tf_op jit(solution)/shard_map/all_gather | solution.py:261
  101.1 1.4 fusion.7
  102.5 0.0 all-reduce.2.cloned.1.call-update
  102.6 55.0 %all-reduce.2.cloned.1.call-done = f32[128,128]{0,1:T(8,128)} async-done(((f32[128,128]{0,1:T(8,128)}), f32[128,128]{0,1:T(8,128)}) %all-reduce.2.cloned.1.call-update) | async-done | bytes 65552 | tf_op jit(solution)/shard_map/psum | solution.py:264
  157.6 0.8 broadcast_multiply_fusion
  158.4 0.1 copy.13
  158.5 0.9 fusion.3
  159.4 11.7 %cholesky.17 = f32[128,128]{1,0:T(8,128)S(1)} custom-call(f32[128,128]{1,0:T(8,128)S(1)} %fusion.3), custom_call_target="Cholesky" | custom-call | tf_op jit(solution)/shard_map/jit(cholesky)/cholesky | solution.py:266
  171.1 0.6 compare_reduce_fusion
  171.8 0.7 fusion
  172.5 9.8 %custom-call.6 = f32[1,128,128]{1,2,0:T(8,128)S(1)} custom-call(f32[1,128,128]{2,1,0:T(8,128)S(1)} %fusion), custom_call_target="InvertDiagBlocksLowerTriangular" | custom-call | tf_op jit(solution)/shard_map/triangular_solve | solution.py:267
  182.3 0.2 fusion.1
  182.5 1.2 fusion.4
  (8 shorter events, 0.1 us)
Async XLA Ops:
  6.5 151.1 %all-reduce.2.cloned.1.call-start = ((), (), s32[]{:S(2)}) async-start(), calls=%async_computation | async-start | bytes 131072 | tf_op jit(solution)/shard_map/psum | solution.py:264
  6.5 28.0 %collective-permute-start.2 = (bf16[6,256,128]{2,1,0:T(8,128)(2,1)}, bf16[6,256,128]{2,1,0:T(8,128)(2,1)S(1)}, u32[]{:S(2)}, u32[]{:S(2)}) collective-permute-start(bf16[6,256,128]{2,1,0:T(8,128)(2,1)} %bitcast.14), channel_id=1, source_target_pairs={{4,0},{8,4},{12,8},{16,12},{20,16},{24,20},{28,24},{5,1},{9,5},{13... | collective-permute-start | bytes 1179656 | tf_op jit(solution)/shard_map/ppermute | solution.py:23
  7.8 26.7 %collective-permute-start = (bf16[6,256,128]{2,1,0:T(8,128)(2,1)}, bf16[6,256,128]{2,1,0:T(8,128)(2,1)S(1)}, u32[]{:S(2)}, u32[]{:S(2)}) collective-permute-start(bf16[6,256,128]{2,1,0:T(8,128)(2,1)} %bitcast.15), channel_id=1, source_target_pairs={{0,4},{4,8},{8,12},{12,16},{16,20},{20,24},{24,28},{1,5},{5,9},{9,... | collective-permute-start | bytes 1179656 | tf_op jit(solution)/shard_map/ppermute | solution.py:23
  11.6 23.0 %collective-permute-start.3 = (bf16[6,1,256]{2,1,0:T(2,128)(2,1)S(1)}, bf16[6,1,256]{2,1,0:T(2,128)(2,1)S(1)}, u32[]{:S(2)}, u32[]{:S(2)}) collective-permute-start(bf16[6,1,256]{2,1,0:T(2,128)(2,1)S(1)} %reshape.21.refs_4_), channel_id=1, source_target_pairs={{4,0},{8,4},{12,8},{16,12},{20,16},{24,20},{28,24},{5,1},{9,5},{13... | collective-permute-start | bytes 9224 | tf_op jit(solution)/shard_map/ppermute | solution.py:23
  12.9 21.7 %collective-permute-start.1 = (bf16[6,1,256]{2,1,0:T(2,128)(2,1)S(1)}, bf16[6,1,256]{2,1,0:T(2,128)(2,1)S(1)}, u32[]{:S(2)}, u32[]{:S(2)}) collective-permute-start(bf16[6,1,256]{2,1,0:T(2,128)(2,1)S(1)} %reshape.21.refs_4_), channel_id=1, source_target_pairs={{0,4},{4,8},{8,12},{12,16},{16,20},{20,24},{24,28},{1,5},{5,9},{9,... | collective-permute-start | bytes 9224 | tf_op jit(solution)/shard_map/ppermute | solution.py:23
  18.0 1.0 copy-start.2
  19.0 0.7 copy-start.4
  19.7 0.7 copy-start.5
  30.6 4.0 %copy-start = (bf16[40,512,256]{2,1,0:T(8,128)(2,1)}, bf16[40,512,256]{2,1,0:T(8,128)(2,1)S(1)}, u32[]{:S(2)}) copy-start(bf16[40,512,256]{2,1,0:T(8,128)(2,1)S(1)} %get-tuple-element.30.tiles) | copy-start | bytes 31457284
  34.6 0.9 copy-start.3
  45.7 11.6 %collective-permute-start.5 = (bf16[6,64,256]{2,1,0:T(8,128)(2,1)S(1)}, bf16[6,64,256]{2,1,0:T(8,128)(2,1)S(1)}, u32[]{:S(2)}, u32[]{:S(2)}) collective-permute-start(bf16[6,64,256]{2,1,0:T(8,128)(2,1)S(1)} %get-tuple-element.26.weighted), channel_id=1, source_target_pairs={{4,0},{8,4},{12,8},{16,12},{20,16},{24,20},{28,24},{5,1},{9,5},{13... | collective-permute-start | bytes 589832 | tf_op jit(solution)/shard_map/ppermute | solution.py:23
  47.0 10.3 %collective-permute-start.4 = (bf16[6,64,256]{2,1,0:T(8,128)(2,1)S(1)}, bf16[6,64,256]{2,1,0:T(8,128)(2,1)S(1)}, u32[]{:S(2)}, u32[]{:S(2)}) collective-permute-start(bf16[6,64,256]{2,1,0:T(8,128)(2,1)S(1)} %get-tuple-element.26.weighted), channel_id=1, source_target_pairs={{0,4},{4,8},{8,12},{12,16},{16,20},{20,24},{24,28},{1,5},{5,9},{9,... | collective-permute-start | bytes 589832 | tf_op jit(solution)/shard_map/ppermute | solution.py:23
  50.1 4.0 %copy-start.1 = (bf16[40,512,256]{2,1,0:T(8,128)(2,1)S(1)}, bf16[40,512,256]{2,1,0:T(8,128)(2,1)}, u32[]{:S(2)}) copy-start(bf16[40,512,256]{2,1,0:T(8,128)(2,1)} %copy-done) | copy-start | bytes 31457284
  60.6 7.6 %collective-permute-start.7 = (bf16[6,64,256]{2,1,0:T(8,128)(2,1)S(1)}, bf16[6,64,256]{2,1,0:T(8,128)(2,1)S(1)}, u32[]{:S(2)}, u32[]{:S(2)}) collective-permute-start(bf16[6,64,256]{2,1,0:T(8,128)(2,1)S(1)} %get-tuple-element.33.weighted), channel_id=1, source_target_pairs={{4,0},{8,4},{12,8},{16,12},{20,16},{24,20},{28,24},{5,1},{9,5},{13... | collective-permute-start | bytes 589832 | tf_op jit(solution)/shard_map/ppermute | solution.py:23
  61.9 6.3 %collective-permute-start.6 = (bf16[6,64,256]{2,1,0:T(8,128)(2,1)S(1)}, bf16[6,64,256]{2,1,0:T(8,128)(2,1)S(1)}, u32[]{:S(2)}, u32[]{:S(2)}) collective-permute-start(bf16[6,64,256]{2,1,0:T(8,128)(2,1)S(1)} %get-tuple-element.33.weighted), channel_id=1, source_target_pairs={{0,4},{4,8},{8,12},{12,16},{16,20},{20,24},{24,28},{1,5},{5,9},{9,... | collective-permute-start | bytes 589832 | tf_op jit(solution)/shard_map/ppermute | solution.py:23
  71.5 7.6 %collective-permute-start.9 = (bf16[6,64,256]{2,1,0:T(8,128)(2,1)S(1)}, bf16[6,64,256]{2,1,0:T(8,128)(2,1)S(1)}, u32[]{:S(2)}, u32[]{:S(2)}) collective-permute-start(bf16[6,64,256]{2,1,0:T(8,128)(2,1)S(1)} %get-tuple-element.35.weighted), channel_id=1, source_target_pairs={{4,0},{8,4},{12,8},{16,12},{20,16},{24,20},{28,24},{5,1},{9,5},{13... | collective-permute-start | bytes 589832 | tf_op jit(solution)/shard_map/ppermute | solution.py:23
  72.8 6.3 %collective-permute-start.8 = (bf16[6,64,256]{2,1,0:T(8,128)(2,1)S(1)}, bf16[6,64,256]{2,1,0:T(8,128)(2,1)S(1)}, u32[]{:S(2)}, u32[]{:S(2)}) collective-permute-start(bf16[6,64,256]{2,1,0:T(8,128)(2,1)S(1)} %get-tuple-element.35.weighted), channel_id=1, source_target_pairs={{0,4},{4,8},{8,12},{12,16},{16,20},{20,24},{24,28},{1,5},{5,9},{9,... | collective-permute-start | bytes 589832 | tf_op jit(solution)/shard_map/ppermute | solution.py:23
Sparse Core Ops, SparseCore 0:
  102.7 54.8 all-reduce.1
where the time goes:
time: 194 us; the launch traced here: 191 us
  waiting for transfers between devices  55.1 us (28%)
  Pallas kernels  40 us (21%)
  other arithmetic  24.6 us (13%)
  starting transfers between devices  23.7 us (12%)
  blocking collectives  18.7 us (10%)
  between operations  13.7 us (7%)
  local copies, waits for them, and re-layouts  12 us (6%)
  matrix products  2.88 us (1%)
    psum x1, waiting for transfers between devices, local(): lax.psum(jnp.dot(flat_vecs, flat_vecs.T, precision=highest), 'rows')  55 us
    ppermute x10, starting transfers between devices, passed_along(): lax.ppermute(value, axis, [(source, source + steps) for source in range(l...  23.7 us
    all_gather x1, blocking collectives, local(): flat_vecs = lax.all_gather(flat, 'cols', axis=0, tiled=True)  18.7 us
    another operation x3, other arithmetic, local(): low_factor = jnp.linalg.cholesky(gram_mat)  12.4 us
    unnamed x12, local copies, waits for them, and re-layouts  11.2 us
    another operation x2, other arithmetic, local(): lax.linalg.triangular_solve(low_factor, jnp.eye(columns, dtype=F32), left...  10.5 us
    pallas_call x1, Pallas kernels, local(): pl.pallas_call(functools.partial(tiles_kernel, True), out_shape=[pltpu.VM...  10.3 us
    pallas_call x1, Pallas kernels, local(): pl.pallas_call(functools.partial(tiles_kernel, False), out_shape=[pltpu.V...  10.2 us
  transfers between devices with their start and end apart: 11, of which 1 were waited for; matrix products, arithmetic and copies ran while one was open for 0% of the time, Pallas kernels for 10%

commit v1 on v0

v1 whole, which is shorter than its diff:
```python
import functools

import jax
import jax.numpy as jnp
from jax import lax
from jax.experimental import pallas as pl
from jax.experimental.pallas import tpu as pltpu
from jax.sharding import PartitionSpec as P

ITERS = 3
GROUP = 4
F32 = jnp.float32
BF16 = jnp.bfloat16
highest = lax.Precision.HIGHEST
MESH = pl.DeviceIdType.MESH
VMEM = pl.BlockSpec(memory_space=pltpu.VMEM)
SMEM = pl.BlockSpec(memory_space=pltpu.SMEM)
NT = (((1,), (1,)), ((), ()))


def split(value):
    high = value.astype(BF16)
    return high, (value - high.astype(F32)).astype(BF16)


def features(emb, left_side):
    size, width = emb.shape
    wide = emb.astype(F32)
    norm = jnp.sum(wide * wide, axis=1, keepdims=True)
    part0 = norm.astype(BF16).astype(F32)
    part1 = (norm - part0).astype(BF16).astype(F32)
    part2 = norm - part0 - part1
    lane = lax.broadcasted_iota(jnp.int32, (size, width), 1)
    base = 3 if left_side else 0
    ones = jnp.where((lane >= 3 - base) & (lane < 6 - base), 1.0, 0.0)
    side = jnp.where(lane == base, -part0, ones)
    side = jnp.where(lane == base + 1, -part1, side)
    side = jnp.where(lane == base + 2, -part2, side)
    main = wide if left_side else 2.0 * wide
    return jnp.concatenate([main.astype(BF16), side.astype(BF16)], axis=1)


def rate_of(spread, width):
    return (1.4426950408889634 / (2.0 * width)) ** 0.5 / spread


def listing(ids, counts, row_here, rows, cols):
    blocks, slots = ids.shape
    first = (row_here - 1) * blocks
    for b in range(blocks):
        rows[b] = b
        cols[b] = blocks + b
    total = jnp.int32(blocks)
    for b in range(blocks):
        count = counts[b]
        for s in range(1, slots):
            rows[total] = b
            cols[total] = ids[b, s] - first
            total = total + jnp.where(s < count, 1, 0)
    for pad in range(GROUP):
        rows[total + pad] = 0
        cols[total + pad] = blocks
    return total


def tiles_kernel(here, ids, counts, emb, spread, emb_l, spread_l, emb_r, spread_r, start,
                 tiles, scale, panel, weighted, rows, cols, groups, left, left_rate, right,
                 right_rate, degree):
    blocks, size, width = emb.shape
    total = listing(ids, counts, here[0], rows, cols)
    groups[0] = (total + GROUP - 1) // GROUP
    position = 0
    for far_emb, far_spread in [(emb_l, spread_l), (emb, spread), (emb_r, spread_r)]:
        for b in range(blocks):
            left[position] = features(far_emb[b], True)
            rate = rate_of(far_spread[b], width)
            left_rate[position] = jnp.broadcast_to(rate, (128, size)).T
            position += 1
    for b in range(blocks):
        right[b] = features(emb[b], False)
        right_rate[b] = rate_of(spread[b], width)

    def tile_of(b, c):
        gap = lax.dot_general(left[c], right[b], NT, preferred_element_type=F32)
        rate = jnp.concatenate([left_rate[c]] * (size // 128), axis=1)
        return jnp.exp2(gap * rate * right_rate[b])

    def keep(t, tile):
        high, low = split(tile)
        tiles[t, :size] = high
        tiles[t, size:] = low
        return jnp.sum(tile, axis=0, keepdims=True)

    apart = lax.broadcasted_iota(jnp.int32, (size, size), 0) != lax.broadcasted_iota(
        jnp.int32, (size, size), 1
    )
    for b in range(blocks):
        degree[b] = keep(b, jnp.where(apart, tile_of(b, blocks + b), 0.0))

    def turn(step, carry):
        first = blocks + 2 * step
        found = []
        for t in (first, first + 1):
            b = rows[t]
            part = keep(t, tile_of(b, cols[t]))
            found.append((b, jnp.where(t < total, part, 0.0)))
        for b, part in found:
            degree[b] += part
        return carry

    lax.fori_loop(0, (total - blocks + 1) // 2, turn, 0)
    for pad in range(GROUP - 1):
        tiles[total + pad] = jnp.zeros((2 * size, size), BF16)
    count = start.shape[0]
    for b in range(blocks):
        factor = 1.0 / jnp.sqrt(degree[b])
        scale[b] = factor
        vecs = start[:, b * size:(b + 1) * size]
        panel[b] = vecs
        high, low = split(vecs * factor)
        weighted[b, :count] = high
        weighted[b, count:] = low


def product_kernel(final, rows, cols, groups, tiles, from_left, own, from_right, scale, panel,
                   *rest):
    if final:
        out, vectors, total = rest
    else:
        out, weighted, vectors, total = rest
    blocks, count, size = panel.shape
    for b in range(blocks):
        vectors[b] = from_left[b]
        vectors[blocks + b] = own[b]
        vectors[2 * blocks + b] = from_right[b]
    total[...] = jnp.zeros(total.shape, F32)

    def one(group, carry):
        found = []
        for place in range(GROUP):
            t = group * GROUP + place
            both = vectors[cols[t]]
            value = jnp.dot(both, tiles[t, :size], preferred_element_type=F32)
            more = jnp.dot(both[:count], tiles[t, size:], preferred_element_type=F32)
            found.append((rows[t], value[:count] + value[count:] + more))
        for b, value in found:
            total[b] += value
        return carry

    lax.fori_loop(0, groups[0], one, 0)
    piece = out.shape[-1]
    for b in range(blocks):
        factor = scale[b]
        vecs = 0.5 * (panel[b] + factor * total[b])
        if final:
            out[:, b * size:(b + 1) * size] = vecs
        else:
            out[b] = vecs
            high, low = split(vecs * factor)
            weighted[b, :count] = high
            weighted[b, count:] = low


def greet(barrier, peers):
    for peer in peers:
        pl.semaphore_signal(barrier, inc=1, device_id=peer, device_id_type=MESH)
    pl.semaphore_wait(barrier, len(peers))


def exchange_kernel(extent, number, *refs):
    values = refs[:number]
    outs = refs[number:3 * number]
    lands = refs[3 * number:5 * number]
    send_sem, recv_sem = refs[5 * number:]
    row, col = lax.axis_index("rows"), lax.axis_index("cols")
    barrier = pltpu.get_barrier_semaphore()
    sides = [(row < extent - 1, row + 1), (row > 0, row - 1)]
    for there, other in sides:
        @pl.when(there)
        def _():
            pl.semaphore_signal(barrier, inc=1, device_id=(other, col), device_id_type=MESH)
    before = jnp.where(row > 0, 1, 0)
    after = jnp.where(row < extent - 1, 1, 0)
    pl.semaphore_wait(barrier, before + after)

    def copy(i, way, other):
        return pltpu.make_async_remote_copy(
            src_ref=values[i], dst_ref=lands[2 * i + way],
            send_sem=send_sem.at[2 * i + way], recv_sem=recv_sem.at[2 * i + way],
            device_id=(other, col), device_id_type=MESH)

    for way, (there, other) in enumerate(sides):
        @pl.when(there)
        def _():
            for i in range(number):
                copy(i, way, other).start()
    for way, (there, other) in enumerate(sides):
        source_there, source = sides[1 - way]

        @pl.when(source_there)
        def _():
            for i in range(number):
                copy(i, way, source).wait_recv()
                outs[2 * i + way][...] = lands[2 * i + way][...]

        @pl.when(jnp.logical_not(source_there))
        def _():
            for i in range(number):
                outs[2 * i + way][...] = jnp.zeros(values[i].shape, values[i].dtype)
    for way, (there, other) in enumerate(sides):
        @pl.when(there)
        def _():
            for i in range(number):
                copy(i, way, other).wait_send()


def exchange(extent, values, collective_id, name):
    number = len(values)
    both = [value for value in values for _ in range(2)]
    return pl.pallas_call(
        functools.partial(exchange_kernel, extent, number),
        out_shape=[jax.ShapeDtypeStruct(v.shape, v.dtype) for v in both],
        in_specs=[VMEM] * number,
        out_specs=[VMEM] * (2 * number),
        scratch_shapes=[pltpu.VMEM(v.shape, v.dtype) for v in both]
        + [pltpu.SemaphoreType.DMA((2 * number,)), pltpu.SemaphoreType.DMA((2 * number,))],
        compiler_params=params(collective_id=collective_id, has_side_effects=True),
        name=name,
    )(*values)


def spread_out(extent, here, at, sources, lands, send_sem, recv_sem):
    copies = []
    for gap in range(1, extent):
        peer = lax.rem(here + gap, extent)
        copies.append(pltpu.make_async_remote_copy(
            src_ref=sources(peer), dst_ref=lands(here), send_sem=send_sem.at[gap - 1],
            recv_sem=recv_sem.at[gap - 1], device_id=at(peer), device_id_type=MESH))
        copies[-1].start()
    for copy in copies:
        copy.wait()


def gram_kernel(row_extent, col_extent, flat, gram_out, turned_out, send, turned, part, part_got,
                block, block_got, whole, last, *sems):
    row, col = lax.axis_index("rows"), lax.axis_index("cols")
    count, points = flat.shape
    piece = points // col_extent
    columns = count * col_extent

    def along_cols(peer):
        return (row, peer)

    def along_rows(peer):
        return (peer, col)

    greet(pltpu.get_barrier_semaphore(),
          [along_cols(lax.rem(col + gap, col_extent)) for gap in range(1, col_extent)]
          + [along_rows(lax.rem(row + gap, row_extent)) for gap in range(1, row_extent)])
    for peer in range(col_extent):
        send[peer] = flat[:, peer * piece:(peer + 1) * piece]
    spread_out(col_extent, col, along_cols, lambda peer: send.at[peer],
               lambda me: turned.at[me], sems[0], sems[1])
    turned[col] = send[col]
    vecs = turned[...].reshape(columns, piece)
    turned_out[...] = vecs
    part[...] = lax.dot_general(
        vecs, vecs, NT, precision=highest, preferred_element_type=F32
    ).reshape(part.shape)
    spread_out(col_extent, col, along_cols, lambda peer: part.at[peer],
               lambda me: part_got.at[me], sems[2], sems[3])
    part_got[col] = part[col]
    block[...] = sum(part_got[peer] for peer in range(col_extent))
    spread_out(row_extent, row, along_rows, lambda peer: block,
               lambda me: block_got.at[me], sems[4], sems[5])
    block_got[row] = block[...]
    last[...] = sum(block_got[peer] for peer in range(row_extent)) / (points * row_extent)
    spread_out(col_extent, col, along_cols, lambda peer: last,
               lambda me: whole.at[me], sems[6], sems[7])
    whole[col] = last[...]
    gram_out[...] = whole[...].reshape(columns, columns)


def inverse_factor(matrix):
    side = matrix.shape[0]
    count = side // 8
    shape = (8, side)
    lane = lax.broadcasted_iota(jnp.int32, shape, 1)
    sub = lax.broadcasted_iota(jnp.int32, shape, 0)
    left = [matrix[8 * g:8 * g + 8] for g in range(count)]
    right = [jnp.where(lane == sub + 8 * g, 1.0, 0.0) for g in range(count)]

    def spread_column(value, j):
        return jnp.broadcast_to(value[:, j:j + 1], shape)

    def spread_row(value, i):
        return jnp.broadcast_to(value[i:i + 1], shape)

    out = []
    for g in range(count):
        first = 8 * g
        column = [spread_column(left[g], first + k) for k in range(8)]
        entry = {(i, k): spread_row(column[k], i) for k in range(8) for i in range(k, 8)}
        inv, mult = [], {}
        for k in range(8):
            inv.append(1.0 / entry[k, k])
            for i in range(k + 1, 8):
                mult[i, k] = entry[i, k] * inv[k]
            for l in range(k + 1, 8):
                for i in range(l, 8):
                    entry[i, l] = entry[i, l] - mult[i, k] * entry[l, k]
        rows = []
        for i in range(8):
            a, w = spread_row(left[g], i), spread_row(right[g], i)
            for k in range(i):
                a = a - mult[i, k] * rows[k][0]
                w = w - mult[i, k] * rows[k][1]
            rows.append((a, w))
        done = jnp.zeros(shape, F32)
        for i in range(8):
            done = jnp.where(sub == i, rows[i][1] * (1.0 / jnp.sqrt(entry[i, i])), done)
        out.append(done)
        solved = [None] * 8
        for i in reversed(range(8)):
            a, w = rows[i][0] * inv[i], rows[i][1] * inv[i]
            for k in range(i + 1, 8):
                a = a - mult[k, i] * solved[k][0]
                w = w - mult[k, i] * solved[k][1]
            solved[i] = (a, w)
        for h in range(g + 1, count):
            a, w = left[h], right[h]
            for k in range(8):
                factor = spread_column(left[h], first + k)
                a = a - factor * solved[k][0]
                w = w - factor * solved[k][1]
            left[h], right[h] = a, w
    return jnp.concatenate(out, axis=0)


def basis_kernel(gram, turned, basis):
    inverse = inverse_factor(gram[...])
    basis[...] = jnp.dot(
        inverse, turned[...], precision=highest, preferred_element_type=F32
    ).reshape(basis.shape)


def return_kernel(col_extent, basis, out, land, send_sem, recv_sem):
    row, col = lax.axis_index("rows"), lax.axis_index("cols")
    piece = basis.shape[-1]

    def along_cols(peer):
        return (row, peer)

    greet(pltpu.get_barrier_semaphore(),
          [along_cols(lax.rem(col + gap, col_extent)) for gap in range(1, col_extent)])
    spread_out(col_extent, col, along_cols, lambda peer: basis.at[peer],
               lambda me: land.at[me], send_sem, recv_sem)
    land[col] = basis[col]
    for peer in range(col_extent):
        out[:, peer * piece:(peer + 1) * piece] = land[peer]


def params(**others):
    return pltpu.CompilerParams(vmem_limit_bytes=12 << 20, **others)


def local(row_extent, col_extent, embeddings, length_scale, start_vectors, neighbour_ids,
          neighbour_counts):
    blocks, slots = neighbour_ids.shape
    points, width = embeddings.shape
    size = points // blocks
    count = start_vectors.shape[0]
    here = lax.axis_index("rows").astype(jnp.int32).reshape(1)
    shape = jax.ShapeDtypeStruct
    dma = pltpu.SemaphoreType.DMA
    emb = embeddings.reshape(blocks, size, width)
    spread = length_scale.astype(F32).reshape(blocks, 1, size)
    emb_l, emb_r, spread_l, spread_r = exchange(row_extent, (emb, spread), 0, "points_exchange")
    most = blocks * slots + GROUP
    block_f32 = shape((blocks, count, size), F32)
    block_both = shape((blocks, 2 * count, size), BF16)
    tiles, scale, panel, weighted, rows, cols, groups = pl.pallas_call(
        tiles_kernel,
        out_shape=[pltpu.VMEM((most, 2 * size, size), BF16), shape((blocks, 1, size), F32),
                   block_f32, block_both, shape((most,), jnp.int32), shape((most,), jnp.int32),
                   shape((1,), jnp.int32)],
        in_specs=[SMEM] * 3 + [VMEM] * 7,
        out_specs=[VMEM] * 4 + [SMEM] * 3,
        scratch_shapes=[
            pltpu.VMEM((3 * blocks, size, 2 * width), BF16),
            pltpu.VMEM((3 * blocks, size, 128), F32),
            pltpu.VMEM((blocks, size, 2 * width), BF16),
            pltpu.VMEM((blocks, 1, size), F32),
            pltpu.VMEM((blocks, 1, size), F32),
        ],
        compiler_params=params(),
        name="tiles",
    )(here, neighbour_ids, neighbour_counts, emb, spread, emb_l, spread_l, emb_r, spread_r,
      start_vectors)

    for iteration in range(ITERS):
        final = iteration == ITERS - 1
        from_left, from_right = exchange(row_extent, (weighted,), 1, "vectors_exchange")
        done = pl.pallas_call(
            functools.partial(product_kernel, final),
            out_shape=[shape((count, points), F32)] if final else [block_f32, block_both],
            in_specs=[SMEM] * 3 + [VMEM] * 6,
            out_specs=[VMEM] if final else [VMEM] * 2,
            scratch_shapes=[pltpu.VMEM((3 * blocks, 2 * count, size), BF16),
                            pltpu.VMEM((blocks, count, size), F32)],
            compiler_params=params(),
            name="product",
        )(rows, cols, groups, tiles, from_left, weighted, from_right, scale, panel)
        if final:
            flat = done[0]
        else:
            panel, weighted = done

    columns = count * col_extent
    piece = points // col_extent
    pieces = pltpu.VMEM((col_extent, count, piece), F32)
    part = pltpu.VMEM((col_extent, count, columns), F32)
    gram, turned = pl.pallas_call(
        functools.partial(gram_kernel, row_extent, col_extent),
        out_shape=[shape((columns, columns), F32), shape((columns, piece), F32)],
        in_specs=[VMEM],
        out_specs=[VMEM] * 2,
        scratch_shapes=[pieces, pieces, part, part, pltpu.VMEM((count, columns), F32),
                        pltpu.VMEM((row_extent, count, columns), F32), part,
                        pltpu.VMEM((count, columns), F32)]
        + [dma((extent - 1,)) for extent in (col_extent, col_extent, row_extent, col_extent)
           for _ in range(2)],
        compiler_params=params(collective_id=2, has_side_effects=True),
        name="gram",
    )(flat)
    basis = pl.pallas_call(
        basis_kernel,
        out_shape=shape((col_extent, count, piece), F32),
        in_specs=[VMEM] * 2,
        out_specs=VMEM,
        compiler_params=params(),
        name="basis",
    )(gram, turned)
    return pl.pallas_call(
        functools.partial(return_kernel, col_extent),
        out_shape=shape((count, points), F32),
        in_specs=[VMEM],
        out_specs=VMEM,
        scratch_shapes=[pieces, dma((col_extent - 1,)), dma((col_extent - 1,))],
        compiler_params=params(collective_id=3, has_side_effects=True),
        name="basis_return",
    )(basis)


def solution(mesh):
    placed = (P("rows", None), P("rows"), P("cols", "rows"), P("rows", None), P("rows"))
    body = functools.partial(local, mesh.shape["rows"], mesh.shape["cols"])
    return jax.shard_map(
        body, mesh=mesh, in_specs=placed, out_specs=P("cols", "rows"), check_vma=False
    )
```

time: 194 us -> 95.4 us (0.49); the launches traced: 191 us -> 93.9 us
  waiting for transfers between devices: 55.1 us -> 0 us
  Pallas kernels: 40 us -> 89.2 us
  other arithmetic: 24.6 us -> 0 us
  starting transfers between devices: 23.7 us -> 0 us
  blocking collectives: 18.7 us -> 0 us
  between operations: 13.7 us -> 0.09 us
  local copies, waits for them, and re-layouts: 12 us -> 4.64 us
  matrix products: 2.88 us -> 0 us
    psum x1 -> x0, waiting for transfers between devices: 55 us -> none  [local(): lax.psum(jnp.dot(flat_vecs, flat_vecs.T, precision=highest), 'rows')]
    pallas_call x8 -> x11, Pallas kernels: 40 us -> 89.2 us  [the longest x4 35.2 us: exchange(): pl.pallas_call(functools.partial(exchange_kernel, extent, number), out_sh...]
    ppermute x10 -> x0, starting transfers between devices: 23.7 us -> none  [passed_along(): lax.ppermute(value, axis, [(source, source + steps) for source in range(l...]
    another operation x5 -> x0, other arithmetic: 22.9 us -> none  [the longest x3 12.4 us: local(): low_factor = jnp.linalg.cholesky(gram_mat)]
    all_gather x1 -> x0, blocking collectives: 18.7 us -> none  [local(): flat_vecs = lax.all_gather(flat, 'cols', axis=0, tiled=True)]
    unnamed x12 -> x9, local copies, waits for them, and re-layouts: 11.2 us -> 3.94 us
    dot_general x2 -> x0, matrix products: 2.63 us -> none  [the longest x1 1.41 us: local(): jnp.dot(flat_vecs, flat_vecs.T, precision=highest)]
  transfers between devices with their start and end apart: 11 -> 0, of which waited for: 1 -> 0; matrix products, arithmetic and copies ran while one was open for 0% -> 0% of each run, Pallas kernels for 10% -> 0%
where the time goes in v1:
time: 95.4 us; the launch traced here: 93.9 us
  Pallas kernels  89.2 us (94%)
  local copies, waits for them, and re-layouts  4.64 us (5%)
    pallas_call x4, Pallas kernels, exchange(): pl.pallas_call(functools.partial(exchange_kernel, extent, number), out_sh...  35.2 us
    pallas_call x1, Pallas kernels, local(): pl.pallas_call(functools.partial(gram_kernel, row_extent, col_extent), ou...  25.9 us
    pallas_call x3, Pallas kernels, local(): pl.pallas_call(functools.partial(product_kernel, final), out_shape=[shape...  9.09 us
    pallas_call x1, Pallas kernels, local(): pl.pallas_call(tiles_kernel, out_shape=[pltpu.VMEM((most, 2 * size, size)...  6.54 us
    pallas_call x1, Pallas kernels, local(): pl.pallas_call(basis_kernel, out_shape=shape((col_extent, count, piece),...  6.35 us
    pallas_call x1, Pallas kernels, local(): pl.pallas_call(functools.partial(return_kernel, col_extent), out_shape=sh...  6.12 us
    unnamed x9, local copies, waits for them, and re-layouts  3.94 us

profile of v1, /device:TPU:0, one launch (start us, length us, event | category | flops | bytes accessed | tf_op | source)
XLA Modules:
  0.0 93.9 jit_solution(11172579871311061267)
XLA Ops:
  0.0 0.7 reshape.16.refs_1_.spread
  0.7 0.0 copy-start
  0.7 1.0 %copy-done = bf16[1536,128]{1,0:T(8,128)(2,1)S(1)} copy-done((bf16[1536,128]{1,0:T(8,128)(2,1)S(1)}, bf16[1536,128]{1,0:T(8,128)(2,1)}, u32[]{:S(2)}) %copy-start) | copy-done | bytes 393240
  1.7 4.4 %points_exchange.1 = (bf16[6,256,128]{2,1,0:T(8,128)(2,1)S(1)}, bf16[6,256,128]{2,1,0:T(8,128)(2,1)S(1)}, f32[6,1,256]{2,1,0:T(1,128)S(1)}, f32[6,1,256]{2,1,0:T(1,128)S(1)}) custom-call(bf16[6,256,128]{2,1,0:T(8,128)(2,1)S(1)} %bitcast.2, f32[6,1,256]{2,1,0:T(1,128)S(1)} %reshape.16.refs_1_.spread), custom_call_target="tpu_custom_call" | custom-call | tf_op jit(solution)/shard_map/points_exchange/pallas_call | solution.py:220
  6.1 0.0 copy-start.1
  6.1 0.9 copy-done.1
  7.0 0.0 copy-start.2
  7.0 0.7 copy-done.2
  7.7 0.0 copy-start.3
  7.7 0.7 copy-done.3
  8.3 6.5 %tiles.1 = (bf16[76,512,256]{2,1,0:T(8,128)(2,1)S(1)}, f32[6,1,256]{2,1,0:T(1,128)S(1)}, f32[6,32,256]{2,1,0:T(8,128)S(1)}, bf16[6,64,256]{2,1,0:T(8,128)(2,1)S(...) custom-call(s32[1]{0:T(128)} %bitcast.here, s32[6,12]{1,0:T(8,128)S(1)} %copy-done.2, s32[6]{0:T(128)S(1)} %copy-done.3, ...), custom_call_target="tpu_custom_call" | custom-call | tf_op jit(solution)/shard_map/tiles/pallas_call | solution.py:382
  14.9 15.1 %vectors_exchange.3 = (bf16[6,64,256]{2,1,0:T(8,128)(2,1)S(1)}, bf16[6,64,256]{2,1,0:T(8,128)(2,1)S(1)}) custom-call(bf16[6,64,256]{2,1,0:T(8,128)(2,1)S(1)} %get-tuple-element.36.refs_0_.own), custom_call_target="tpu_custom_call" | custom-call | tf_op jit(solution)/shard_map/vectors_exchange/pallas_call | solution.py:220
  30.0 3.0 %product.3 = (f32[6,32,256]{2,1,0:T(8,128)S(1)}, bf16[6,64,256]{2,1,0:T(8,128)(2,1)S(1)}) custom-call(s32[76]{0:T(128)S(1)} %get-tuple-element.32.rows, s32[76]{0:T(128)S(1)} %get-tuple-element.33.cols, s32[1]{0:T(128)} %get-tuple-element.34.groups, bf16[76,512,256]{2,1,0:T(8,128)(2,1)S(1)} %get-tuple-element.35.tiles, ...), custom_call_target="tpu_custom_call" | custom-call | tf_op jit(solution)/shard_map/product/pallas_call | solution.py:404
  33.1 7.9 %vectors_exchange.4 = (bf16[6,64,256]{2,1,0:T(8,128)(2,1)S(1)}, bf16[6,64,256]{2,1,0:T(8,128)(2,1)S(1)}) custom-call(bf16[6,64,256]{2,1,0:T(8,128)(2,1)S(1)} %get-tuple-element.41.refs_0_.own), custom_call_target="tpu_custom_call" | custom-call | tf_op jit(solution)/shard_map/vectors_exchange/pallas_call | solution.py:220
  40.9 3.0 %product.4 = (f32[6,32,256]{2,1,0:T(8,128)S(1)}, bf16[6,64,256]{2,1,0:T(8,128)(2,1)S(1)}) custom-call(s32[76]{0:T(128)S(1)} %get-tuple-element.32.rows, s32[76]{0:T(128)S(1)} %get-tuple-element.33.cols, s32[1]{0:T(128)} %get-tuple-element.34.groups, bf16[76,512,256]{2,1,0:T(8,128)(2,1)S(1)} %get-tuple-element.35.tiles, ...), custom_call_target="tpu_custom_call" | custom-call | tf_op jit(solution)/shard_map/product/pallas_call | solution.py:404
  44.0 7.9 %vectors_exchange.5 = (bf16[6,64,256]{2,1,0:T(8,128)(2,1)S(1)}, bf16[6,64,256]{2,1,0:T(8,128)(2,1)S(1)}) custom-call(bf16[6,64,256]{2,1,0:T(8,128)(2,1)S(1)} %get-tuple-element.45.refs_0_.own), custom_call_target="tpu_custom_call" | custom-call | tf_op jit(solution)/shard_map/vectors_exchange/pallas_call | solution.py:220
  51.9 3.0 %product.5.flat = f32[32,1536]{1,0:T(8,128)S(1)} custom-call(s32[76]{0:T(128)S(1)} %get-tuple-element.32.rows, s32[76]{0:T(128)S(1)} %get-tuple-element.33.cols, s32[1]{0:T(128)} %get-tuple-element.34.groups, bf16[76,512,256]{2,1,0:T(8,128)(2,1)S(1)} %get-tuple-element.35.tiles, bf16[6,64,256]{2,1,0:T(8,128)(2,1)S(1)} %get-tuple-element.46.from_left, ...), custom_call_target="tpu_custom_call" | custom-call | tf_op jit(solution)/shard_map/product/pallas_call | solution.py:404
  54.9 25.9 %gram.1 = (f32[128,128]{1,0:T(8,128)S(1)}, f32[128,384]{1,0:T(8,128)S(1)}) custom-call(f32[32,1536]{1,0:T(8,128)S(1)} %product.5.flat), custom_call_target="tpu_custom_call" | custom-call | tf_op jit(solution)/shard_map/gram/pallas_call | solution.py:423
  80.8 6.4 %basis.1 = f32[4,32,384]{2,1,0:T(8,128)S(1)} custom-call(f32[128,128]{1,0:T(8,128)S(1)} %get-tuple-element.49.gram, f32[128,384]{1,0:T(8,128)S(1)} %get-tuple-element.50.turned), custom_call_target="tpu_custom_call" | custom-call | tf_op jit(solution)/shard_map/basis/pallas_call | solution.py:436
  87.1 6.1 %basis_return.1 = f32[32,1536]{1,0:T(8,128)S(1)} custom-call(f32[4,32,384]{2,1,0:T(8,128)S(1)} %basis.1), custom_call_target="tpu_custom_call" | custom-call | tf_op jit(solution)/shard_map/basis_return/pallas_call | solution.py:444
  93.3 0.7 copy.7
Async XLA Ops:
  0.7 1.0 %copy-start = (bf16[1536,128]{1,0:T(8,128)(2,1)S(1)}, bf16[1536,128]{1,0:T(8,128)(2,1)}, u32[]{:S(2)}) copy-start(bf16[1536,128]{1,0:T(8,128)(2,1)} %param.5) | copy-start | bytes 1179652
  6.1 0.9 copy-start.1
  7.0 0.7 copy-start.2
  7.7 0.7 copy-start.3
